TPU v7x, 512 devices: a whole 4x4x16 slice. The times are simulated.
512 devices in a mesh: ctx: 64 (over z, x_lo, core), ch: 8 (over x_hi, y).
Axes of the slice: x: 4 (x_hi: 2, x_lo: 2; x = x_hi * 2 + x_lo), y: 4, z: 16, core: 2. Of those that a mesh axis runs over, the one named last changes fastest.
Arguments:
- q_in: bfloat16 [8192, 8192], P('ctx', 'ch'), may hold values from -6 to 6
- k_in: bfloat16 [8192, 8192], P('ctx', 'ch'), may hold values from -6 to 6
- v_in: bfloat16 [8192, 8192], P('ctx', 'ch'), may hold values from -6 to 6
- stretch_of_slot: int32 [128], replicated, may hold values from 0 to 127, each once
- short_weight: float32 [3, 7, 8192], P(None, None, 'ch'), may hold values from -2 to 2
- rates: float32 [16, 8192], P(None, 'ch'), may hold values from 1.2207031e-06 to 0.03
- residues: float32 [16, 8192], P(None, 'ch'), may hold values from -12 to 12
- skip: float32 [8192], P('ch'), may hold values from -4 to 4
- gain: float32 [8192], P('ch'), may hold values from 0.5 to 1.5
Outputs:
- operator_out: bfloat16 [8192, 8192], P('ctx', 'ch')
Inputs may be any that keep to these rules, and one draw needn't show every extreme that they name: stretch_of_slot names every sequence stretch exactly once.
All inputs are finite; a program needn't handle non-finite values.
Results may differ from a plain program's by a relative error of at most 0.001.
Values may be sent and summed in bfloat16 or wider, within the bound.
A program may use at most 64 MiB of HBM per device.

v0:
```python
import jax
import jax.numpy as jnp
from jax import lax
from jax.sharding import PartitionSpec as P

D = 8192


def decay_combine(earlier, later):
    return (earlier[0] * later[0], earlier[1] * later[0] + later[1])


def on_device(q_in, k_in, v_in, stretch_of_slot, short_weight, rates, residues, skip, gain):
    tokens, width = q_in.shape
    stretch = tokens // 2
    reach = short_weight.shape[1] - 1
    order = rates.shape[0]
    span = float(stretch)
    my_index = lax.axis_index("ctx")
    own_stretches = lax.dynamic_slice_in_dim(stretch_of_slot, 2 * my_index, 2)
    stacked = jnp.stack([q_in, k_in, v_in]).reshape(3, 2, stretch, width)
    tail_rows = (
        stacked[:, :, stretch - reach :, :].transpose(1, 0, 2, 3).reshape(2, 3 * reach, width)
    )
    stretch_ids = stretch_of_slot
    select = (stretch_ids[None, :] == own_stretches[:, None] - 1).astype(jnp.bfloat16)
    previous = jnp.einsum(
        "mn,nxw->mxw",
        select,
        lax.all_gather(tail_rows, "ctx", axis=0, tiled=True),
        preferred_element_type=jnp.float32,
    )
    previous = previous.reshape(2, 3, reach, width).transpose(1, 0, 2, 3)
    extended = jnp.concatenate([previous, stacked.astype(jnp.float32)], axis=2)
    features = jnp.zeros((3, 2, stretch, width), jnp.float32)
    for shift_by in range(reach + 1):
        features = (
            features
            + short_weight[:, shift_by][:, None, None, :]
            * extended[:, :, reach - shift_by : reach - shift_by + stretch, :]
        )
    query = features[0]
    mixed_in = features[1] * features[2]
    positions = jnp.arange(stretch, dtype=jnp.float32)
    scaled = residues * jnp.sqrt(-jnp.expm1(-2.0 * rates))

    def mode_pass(mode, state):
        local_conv, ends = state
        rate = lax.dynamic_index_in_dim(rates, mode, 0, keepdims=False)
        amount = lax.dynamic_index_in_dim(scaled, mode, 0, keepdims=False)
        factors = jnp.broadcast_to(jnp.exp(-rate)[None, None, :], mixed_in.shape)
        running = lax.associative_scan(decay_combine, (factors, mixed_in), axis=1)[1]
        local_conv = local_conv + amount[None, None, :] * running
        ends = lax.dynamic_update_index_in_dim(ends, running[:, stretch - 1 : stretch, :], mode, 1)
        return (local_conv, ends)

    local_conv, ends = lax.fori_loop(
        0,
        order,
        mode_pass,
        (jnp.zeros((2, stretch, width), jnp.float32), jnp.zeros((2, order, width), jnp.float32)),
    )
    pieces = lax.all_gather(ends, "ctx", axis=0, tiled=True)
    stretch_ids = stretch_of_slot

    def one_target(target):
        gaps = target - 1 - stretch_ids
        before = gaps >= 0
        steps_back = jnp.maximum(gaps, 0).astype(jnp.float32)
        weights = jnp.where(
            before[:, None, None], jnp.exp(-rates[None] * (span * steps_back[:, None, None])), 0.0
        )
        return jnp.sum(weights * pieces, axis=0)

    starts = lax.map(one_target, own_stretches)

    def carry_pass(mode, total):
        rate = lax.dynamic_index_in_dim(rates, mode, 0, keepdims=False)
        amount = lax.dynamic_index_in_dim(scaled, mode, 0, keepdims=False)
        lifted = jnp.exp(-rate[None, :] * (positions[:, None] + 1.0))
        begin = lax.dynamic_index_in_dim(starts, mode, 1, keepdims=False)
        return total + (amount[None, :] * lifted)[None] * begin[:, None, :]

    carried = lax.fori_loop(0, order, carry_pass, jnp.zeros((2, stretch, width), jnp.float32))
    output = local_conv + carried + skip[None, None, :] * mixed_in
    zvalues = query * output
    squares = lax.psum(jnp.sum(zvalues * zvalues, axis=-1), "ch")
    scale = lax.rsqrt(squares / D + 1e-05)
    normed = (zvalues * scale[:, :, None] * gain[None, None, :]).astype(jnp.bfloat16)
    return normed.reshape(tokens, width)


def solution(mesh):
    in_specs = (
        P("ctx", "ch"),
        P("ctx", "ch"),
        P("ctx", "ch"),
        P(),
        P(None, None, "ch"),
        P(None, "ch"),
        P(None, "ch"),
        P("ch"),
        P("ch"),
    )
    out_specs = P("ctx", "ch")
    return jax.shard_map(
        on_device, mesh=mesh, in_specs=in_specs, out_specs=out_specs, check_vma=False
    )
```

profile of v0, /device:TPU:32, one launch (start us, length us, event | category | flops | bytes accessed | tf_op | source)
XLA Modules:
  0.0 368.7 jit_solution(7288362771378136959)
XLA Ops:
  6.5 1.3 pad_maximum_fusion.6
  8.0 0.7 copy.21
  9.0 130.6 %all-gather.3.cloned.1.call-done = bf16[128,18,1024]{2,1,0:T(8,128)(2,1)} async-done(((bf16[2,18,1024]{2,1,0:T(8,128)(2,1)}), bf16[128,18,1024]{2,1,0:T(8,128)(2,1)}) %all-gather.3.cloned.1.call-update) | async-done | bytes 4718608 | tf_op jit(solution)/shard_map/all_gather | solution.py:30
  139.6 7.8 %fusion.8 = f32[2,18,1024]{2,0,1:T(2,128)S(1)} fusion(bf16[128,18,1024]{2,1,0:T(8,128)(2,1)} %all-gather.3.cloned.1.call-done, s32[128]{0:T(128)S(1)} %copy-done.8, s32[2]{0:T(128)S(1)} %get-tuple-element.404), kind=kOutput, calls=%fused_computation.44 | convolution fusion | flops 9437440 | bytes 4866568 | tf_op jit(solution)/shard_map/mn,nxw->mxw/dot_general | solution.py:27
  147.5 1.4 fusion.13
  148.9 1.2 copy-done
  150.2 43.7 %while.43 = (s32[]{:T(128)}, f32[2,64,1024]{2,1,0:T(8,128)S(1)}, f32[2,16,1024]{2,1,0:T(8,128)S(1)}, f32[16,1024]{1,0:T(8,128)S(1)}, f32[2,64,1024]{2,1,0:T(8,12...) while((s32[]{:T(128)}, f32[2,64,1024]{2,1,0:T(8,128)S(1)}, ...), condition=%wide.region_1.2_spmd.clone, body=%wide.region_0.1_spmd.clone.sunk | while | flops 1394691 | bytes 14254231 | solution.py:57
  152.1 0.2 slice.590
  152.6 0.3 select_add_fusion.4
  154.8 0.2 slice.590
  155.4 0.3 select_add_fusion.4
  157.5 0.2 slice.590
  158.1 0.3 select_add_fusion.4
  160.3 0.2 slice.590
  160.8 0.3 select_add_fusion.4
  163.0 0.2 slice.590
  163.6 0.3 select_add_fusion.4
  165.7 0.2 slice.590
  166.3 0.3 select_add_fusion.4
  168.5 0.2 slice.590
  169.0 0.3 select_add_fusion.4
  171.2 0.2 slice.590
  171.8 0.3 select_add_fusion.4
  173.9 0.2 slice.590
  174.5 0.3 select_add_fusion.4
  176.7 0.2 slice.590
  177.2 0.3 select_add_fusion.4
  179.4 0.2 slice.590
  180.0 0.3 select_add_fusion.4
  182.1 0.2 slice.590
  182.7 0.3 select_add_fusion.4
  184.9 0.2 slice.590
  185.4 0.3 select_add_fusion.4
  187.6 0.2 slice.590
  188.2 0.3 select_add_fusion.4
  190.9 0.3 select_add_fusion.4
  193.6 0.3 select_add_fusion.4
  194.0 0.6 copy-done.2
  194.6 124.3 %all-gather.5.cloned.1.call-done = f32[128,16,1024]{2,1,0:T(8,128)} async-done(((f32[2,16,1024]{2,1,0:T(8,128)}), f32[128,16,1024]{2,1,0:T(8,128)}) %all-gather.5.cloned.1.call-update) | async-done | bytes 8388624 | tf_op jit(solution)/shard_map/all_gather | solution.py:63
  318.9 11.6 %while.42 = (s32[]{:T(128)}, f32[2,16,1024]{2,1,0:T(8,128)S(1)}, s32[2]{0:T(128)S(1)}, s32[128]{0:T(128)S(1)}, f32[1,16,1024]{2,1,0:T(8,128)S(1)}, /*index=5*/f32[128,16,1024]{2,1,0:T(8,128)}, s32[]{:T(128)}, s32[1]{0:T(128)}) while((s32[]{:T(128)}, f32[2,16,1024]{2,1,0:T(8,128)S(1)}, s32[2]{0:T(128)S(1)}, s32[128]{0:T(128)S(1)}, ...), condition=%wide.region_4.5_spmd, body=%wide.region_2.4_spmd.sunk | while | flops 8372995 | bytes 8653177 | solution.py:75
  318.9 0.6 dynamic_slice.66
  320.2 4.5 %multiply_reduce_fusion.3 = f32[16,1024]{1,0:T(8,128)S(1)} fusion(f32[128,16,1024]{2,1,0:T(8,128)} %get-tuple-element.615, f32[128]{0:T(128)S(1)} %convert_multiply_fusion.2, f32[16,1024]{1,0:T(8,128)S(1)} %bitcast.67, pred[128]{0:T(512)(128)(4,1)S(1)} %subtract_compare_fusion.2), kind=kLoop, calls=%fused_computation.1.clone.1 | loop fusion | flops 8372224 | bytes 8520320 | tf_op jit(solution)/shard_map/while/body/eval_jaxpr/reduce_sum | solution.py:73
  324.7 0.6 dynamic_slice.66
  326.0 4.5 %multiply_reduce_fusion.3 = f32[16,1024]{1,0:T(8,128)S(1)} fusion(f32[128,16,1024]{2,1,0:T(8,128)} %get-tuple-element.615, f32[128]{0:T(128)S(1)} %convert_multiply_fusion.2, f32[16,1024]{1,0:T(8,128)S(1)} %bitcast.67, pred[128]{0:T(512)(128)(4,1)S(1)} %subtract_compare_fusion.2), kind=kLoop, calls=%fused_computation.1.clone.1 | loop fusion | flops 8372224 | bytes 8520320 | tf_op jit(solution)/shard_map/while/body/eval_jaxpr/reduce_sum | solution.py:73
  330.5 6.2 %while.44 = (s32[]{:T(128)}, f32[2,64,1024]{2,1,0:T(8,128)S(1)}, f32[16,1024]{1,0:T(8,128)S(1)}, f32[16,1024]{1,0:T(8,128)S(1)}, f32[2,16,1024]{2,1,0:T(8,128)S(1)}, /*index=5*/s32[]{:T(128)}, s32[]{:T(128)}) while((s32[]{:T(128)}, f32[2,64,1024]{2,1,0:T(8,128)S(1)}, f32[16,1024]{1,0:T(8,128)S(1)}, f32[16,1024]{1,0:T(8,128)S(1)}, ...), condition=%wide.region_6.7_spmd.clone, body=%wide.region_5.6_spmd.clone.sunk | while | flops 525379 | bytes 1639007 | solution.py:84
  330.7 0.2 select_add_fusion.5
  331.1 0.2 select_add_fusion.5
  331.5 0.2 select_add_fusion.5
  331.9 0.2 select_add_fusion.5
  332.3 0.2 select_add_fusion.5
  332.6 0.2 select_add_fusion.5
  333.0 0.2 select_add_fusion.5
  333.4 0.2 select_add_fusion.5
  333.8 0.2 select_add_fusion.5
  334.2 0.2 select_add_fusion.5
  334.6 0.2 select_add_fusion.5
  335.0 0.2 select_add_fusion.5
  335.3 0.2 select_add_fusion.5
  335.7 0.2 select_add_fusion.5
  336.1 0.2 select_add_fusion.5
  336.5 0.2 select_add_fusion.5
  336.7 0.2 multiply_reduce_fusion.1
  336.9 24.1 %psum.7 = f32[2,64]{1,0:T(2,128)S(1)} all-reduce(f32[2,64]{1,0:T(2,128)S(1)} %get-tuple-element.402), channel_id=1, replica_groups=mesh['ctx'=64,'ch'=8] {'ch'}, use_global_device_ids=true, to_apply=%region_8.9 | all-reduce | flops 128 | bytes 1024 | tf_op jit(solution)/shard_map/psum | solution.py:87
  361.0 0.8 multiply_convert_fusion
  (956 shorter events, 33.9 us)
Async XLA Ops:
  6.5 133.1 %all-gather.3.cloned.1.call-start = ((), (), s32[]{:S(2)}) async-start(), calls=%async_computation | async-start | bytes 6389760 | tf_op jit(solution)/shard_map/all_gather | solution.py:30
  6.5 2.2 copy-start.4
  6.5 2.3 copy-start.8
  6.5 2.4 copy-start.3
  6.5 2.4 copy-start.5
  8.7 310.2 %all-gather.5.cloned.1.call-start = ((), (), s32[]{:S(2)}) async-start(), calls=%async_computation.1 | async-start | bytes 8519680 | tf_op jit(solution)/shard_map/all_gather | solution.py:63
  148.9 1.2 copy-start
  193.9 0.7 copy-start.2
  330.5 6.2 %copy-start.1 = (f32[3,2,64,1024]{3,2,1,0:T(8,128)S(1)}, f32[3,2,64,1024]{3,2,1,0:T(8,128)}, u32[]{:S(2)}) copy-start(f32[3,2,64,1024]{3,2,1,0:T(8,128)} %copy-done) | copy-start | bytes 4718596
  330.5 6.2 %copy-start.6 = (f32[1024]{0:T(1024)S(1)}, f32[1024]{0:T(1024)}, u32[]{:S(2)}) copy-start(f32[1024]{0:T(1024)} %param.22) | copy-start | bytes 12292
  336.7 24.3 %copy-start.7 = (f32[1024]{0:T(1024)S(1)}, f32[1024]{0:T(1024)}, u32[]{:S(2)}) copy-start(f32[1024]{0:T(1024)} %param.23) | copy-start | bytes 12292
Sparse Core Ops, SparseCore 0:
  9.5 130.1 all-gather.2
  194.7 124.0 all-gather.4
where the time goes:
time: 369 us
  waiting for transfers between devices  255 us (69%)
  other arithmetic  30.7 us (8%)
  local copies, waits for them, and re-layouts  29.6 us (8%)
  blocking collectives  24.1 us (7%)
  between operations  13.6 us (4%)
  loops' own time  8.04 us (2%)
  matrix products  7.8 us (2%)
    all_gather x1, waiting for transfers between devices, on_device(): lax.all_gather(tail_rows, 'ctx', axis=0, tiled=True)  131 us
    all_gather x1, waiting for transfers between devices, on_device(): pieces = lax.all_gather(ends, 'ctx', axis=0, tiled=True)  124 us
    psum x1, blocking collectives, on_device(): squares = lax.psum(jnp.sum(zvalues * zvalues, axis=-1), 'ch')  24.1 us
    slice x288, local copies, waits for them, and re-layouts, mode_pass(): lax.associative_scan(decay_combine, (factors, mixed_in), axis=1)[1]  13.9 us
    pad x160, local copies, waits for them, and re-layouts, mode_pass(): lax.associative_scan(decay_combine, (factors, mixed_in), axis=1)[1]  9.36 us
    reduce_sum x2, other arithmetic, one_target(): return jnp.sum(weights * pieces, axis=0)  8.94 us
    dot_general x1, matrix products, on_device(): jnp.einsum('mn,nxw->mxw', select, lax.all_gather(tail_rows, 'ctx', axis=0...  7.8 us
  transfers between devices with their start and end apart: 2, of which 2 were waited for; matrix products, arithmetic and copies ran while one was open for 0% of the time, Pallas kernels for 0%

commit v1 on v0

--- a/solution.py
+++ b/solution.py
@@ -27,7 +27,9 @@
     previous = jnp.einsum(
         "mn,nxw->mxw",
         select,
-        lax.all_gather(tail_rows, "ctx", axis=0, tiled=True),
+        jnp.concatenate(
+            lax.all_to_all(jnp.stack([tail_rows] * lax.axis_size("ctx")), "ctx", 0, 0), axis=0
+        ),
         preferred_element_type=jnp.float32,
     )
     previous = previous.reshape(2, 3, reach, width).transpose(1, 0, 2, 3)

time: 369 us -> 480 us (1.30)
  waiting for transfers between devices: 255 us -> 332 us
  local copies, waits for them, and re-layouts: 29.6 us -> 50.7 us
  starting transfers between devices: 0.04 us -> 17.2 us
    all_to_all x0 -> x1, waiting for transfers between devices: none -> 210 us  [on_device(): lax.all_to_all(jnp.stack([tail_rows] * lax.axis_size('ctx')), 'ctx', 0, 0)]
    all_gather x1 -> x0, waiting for transfers between devices: 131 us -> none  [on_device(): lax.all_gather(tail_rows, 'ctx', axis=0, tiled=True)]
    all_to_all x0 -> x1, starting transfers between devices: none -> 17 us  [on_device(): lax.all_to_all(jnp.stack([tail_rows] * lax.axis_size('ctx')), 'ctx', 0, 0)]
    all_to_all x0 -> x1, local copies, waits for them, and re-layouts: none -> 9.11 us  [on_device(): lax.all_to_all(jnp.stack([tail_rows] * lax.axis_size('ctx')), 'ctx', 0, 0)]
    reshape x2 -> x1, local copies, waits for them, and re-layouts: 0.71 us -> 8.06 us  [on_device(): jnp.concatenate(lax.all_to_all(jnp.stack([tail_rows] * lax.axis_size('ctx...]
where the time goes in v1:
time: 480 us
  waiting for transfers between devices  332 us (69%)
  local copies, waits for them, and re-layouts  50.7 us (11%)
  other arithmetic  30.6 us (6%)
  blocking collectives  24.1 us (5%)
  starting transfers between devices  17.2 us (4%)
  between operations  13.6 us (3%)
  loops' own time  8.04 us (2%)
    all_to_all x1, waiting for transfers between devices, on_device(): lax.all_to_all(jnp.stack([tail_rows] * lax.axis_size('ctx')), 'ctx', 0, 0)  210 us
    all_gather x1, waiting for transfers between devices, on_device(): pieces = lax.all_gather(ends, 'ctx', axis=0, tiled=True)  122 us
    psum x1, blocking collectives, on_device(): squares = lax.psum(jnp.sum(zvalues * zvalues, axis=-1), 'ch')  24.1 us
    all_to_all x1, starting transfers between devices, on_device(): lax.all_to_all(jnp.stack([tail_rows] * lax.axis_size('ctx')), 'ctx', 0, 0)  17 us
    slice x288, local copies, waits for them, and re-layouts, mode_pass(): lax.associative_scan(decay_combine, (factors, mixed_in), axis=1)[1]  13.9 us
  transfers between devices with their start and end apart: 2, of which 2 were waited for; matrix products, arithmetic and copies ran while one was open for 0% of the time, Pallas kernels for 0%

profile of v1, /device:TPU:32, one launch (start us, length us, event | category | flops | bytes accessed | tf_op | source)
XLA Modules:
  0.0 479.8 jit_solution(17824539209110383332)
XLA Ops:
  6.5 1.3 pad_maximum_fusion.6
  7.9 4.6 stack.19
  12.5 17.0 %all-to-all-start = ((bf16[64,2,18,1024]{3,1,2,0:T(2,128)(2,1)}), bf16[64,2,18,1024]{3,1,2,0:T(2,128)(2,1)}, u32[]{:S(2)}, u32[]{:S(2)}) async-start(bf16[64,2,18,1024]{3,1,2,0:T(2,128)(2,1)} %stack.19), calls=%async_computation | async-start | bytes 9437184 | tf_op jit(solution)/shard_map/all_to_all | solution.py:31
  29.5 0.2 all-gather.2.cloned.1.call-start
  30.1 209.9 %all-to-all-done = bf16[64,2,18,1024]{3,1,2,0:T(2,128)(2,1)} async-done(((bf16[64,2,18,1024]{3,1,2,0:T(2,128)(2,1)}), bf16[64,2,18,1024]{3,1,2,0:T(2,128)(2,1)}, u32[]{:S(2)}, u32[]{:S(2)}) %all-to-all-start) | async-done | bytes 4718624 | tf_op jit(solution)/shard_map/all_to_all | solution.py:31
  240.0 9.1 %copy.17 = bf16[64,2,18,1024]{3,1,0,2:T(2,128)(2,1)} copy(bf16[64,2,18,1024]{3,1,2,0:T(2,128)(2,1)} %all-to-all-done) | data formatting | bytes 9437184 | tf_op jit(solution)/shard_map/all_to_all | solution.py:31
  249.1 8.1 %reshape.121 = bf16[128,18,1024]{2,0,1:T(8,128)(2,1)} reshape(bf16[64,2,18,1024]{3,1,0,2:T(2,128)(2,1)} %copy.17) | data formatting | bytes 9437184 | tf_op jit(solution)/shard_map/reshape | solution.py:30
  257.2 3.1 convolution_bitcast_fusion
  260.4 1.4 fusion.11
  261.8 1.2 copy-done
  263.1 43.7 %while.43 = (s32[]{:T(128)}, f32[2,64,1024]{2,1,0:T(8,128)S(1)}, f32[2,16,1024]{2,1,0:T(8,128)S(1)}, f32[16,1024]{1,0:T(8,128)S(1)}, f32[2,64,1024]{2,1,0:T(8,12...) while((s32[]{:T(128)}, f32[2,64,1024]{2,1,0:T(8,128)S(1)}, ...), condition=%wide.region_1.2_spmd.clone, body=%wide.region_0.1_spmd.clone.sunk | while | flops 1394691 | bytes 14254231 | solution.py:59
  265.0 0.2 slice.590
  265.5 0.3 select_add_fusion.4
  267.7 0.2 slice.590
  268.3 0.3 select_add_fusion.4
  270.4 0.2 slice.590
  271.0 0.3 select_add_fusion.4
  273.2 0.2 slice.590
  273.7 0.3 select_add_fusion.4
  275.9 0.2 slice.590
  276.5 0.3 select_add_fusion.4
  278.6 0.2 slice.590
  279.2 0.3 select_add_fusion.4
  281.9 0.3 select_add_fusion.4
  284.7 0.3 select_add_fusion.4
  287.4 0.3 select_add_fusion.4
  290.1 0.3 select_add_fusion.4
  292.3 0.2 slice.590
  292.9 0.3 select_add_fusion.4
  295.0 0.2 slice.590
  295.6 0.3 select_add_fusion.4
  297.8 0.2 slice.590
  298.3 0.3 select_add_fusion.4
  300.5 0.2 slice.590
  301.1 0.3 select_add_fusion.4
  303.8 0.3 select_add_fusion.4
  306.5 0.3 select_add_fusion.4
  306.9 0.6 copy-done.2
  307.5 122.4 %all-gather.2.cloned.1.call-done = f32[128,16,1024]{2,1,0:T(8,128)} async-done(((f32[2,16,1024]{2,1,0:T(8,128)}), f32[128,16,1024]{2,1,0:T(8,128)}) %all-gather.2.cloned.1.call-update) | async-done | bytes 8388624 | tf_op jit(solution)/shard_map/all_gather | solution.py:65
  430.0 11.6 %while.42 = (s32[]{:T(128)}, f32[2,16,1024]{2,1,0:T(8,128)S(1)}, s32[2]{0:T(128)S(1)}, s32[128]{0:T(128)S(1)}, f32[1,16,1024]{2,1,0:T(8,128)S(1)}, /*index=5*/f32[128,16,1024]{2,1,0:T(8,128)}, s32[]{:T(128)}, s32[1]{0:T(128)}) while((s32[]{:T(128)}, f32[2,16,1024]{2,1,0:T(8,128)S(1)}, s32[2]{0:T(128)S(1)}, s32[128]{0:T(128)S(1)}, ...), condition=%wide.region_4.5_spmd, body=%wide.region_2.4_spmd.sunk | while | flops 8372995 | bytes 8653177 | solution.py:77
  430.0 0.6 dynamic_slice.66
  431.2 4.5 multiply_reduce_fusion.3
  435.8 0.6 dynamic_slice.66
  437.0 4.5 multiply_reduce_fusion.3
  441.5 6.2 %while.44 = (s32[]{:T(128)}, f32[2,64,1024]{2,1,0:T(8,128)S(1)}, f32[16,1024]{1,0:T(8,128)S(1)}, f32[16,1024]{1,0:T(8,128)S(1)}, f32[2,16,1024]{2,1,0:T(8,128)S(1)}, /*index=5*/s32[]{:T(128)}, s32[]{:T(128)}) while((s32[]{:T(128)}, f32[2,64,1024]{2,1,0:T(8,128)S(1)}, f32[16,1024]{1,0:T(8,128)S(1)}, f32[16,1024]{1,0:T(8,128)S(1)}, ...), condition=%wide.region_6.7_spmd.clone, body=%wide.region_5.6_spmd.clone.sunk | while | flops 525379 | bytes 1639007 | solution.py:86
  441.8 0.2 select_add_fusion.5
  442.1 0.2 select_add_fusion.5
  442.5 0.2 select_add_fusion.5
  442.9 0.2 select_add_fusion.5
  443.3 0.2 select_add_fusion.5
  443.7 0.2 select_add_fusion.5
  444.1 0.2 select_add_fusion.5
  444.5 0.2 select_add_fusion.5
  444.9 0.2 select_add_fusion.5
  445.2 0.2 select_add_fusion.5
  445.6 0.2 select_add_fusion.5
  446.0 0.2 select_add_fusion.5
  446.4 0.2 select_add_fusion.5
  446.8 0.2 select_add_fusion.5
  447.2 0.2 select_add_fusion.5
  447.6 0.2 select_add_fusion.5
  447.8 0.2 multiply_reduce_fusion.1
  448.0 24.1 %psum.7 = f32[2,64]{1,0:T(2,128)S(1)} all-reduce(f32[2,64]{1,0:T(2,128)S(1)} %get-tuple-element.397), channel_id=1, replica_groups=mesh['ctx'=64,'ch'=8] {'ch'}, use_global_device_ids=true, to_apply=%region_8.9 | all-reduce | flops 128 | bytes 1024 | tf_op jit(solution)/shard_map/psum | solution.py:89
  472.1 0.8 multiply_convert_fusion
  (957 shorter events, 34.5 us)
Async XLA Ops:
  12.5 17.3 %copy-start.4 = (f32[3,7,1024]{2,1,0:T(8,128)S(1)}, f32[3,7,1024]{2,1,0:T(8,128)}, u32[]{:S(2)}) copy-start(f32[3,7,1024]{2,1,0:T(8,128)} %param.19) | copy-start | bytes 258052
  12.5 17.4 %copy-start.8 = (s32[128]{0:T(128)S(1)}, s32[128]{0:T(128)}, u32[]{:S(2)}) copy-start(s32[128]{0:T(128)} %param.18) | copy-start | bytes 1540
  12.5 17.5 %copy-start.3 = (f32[16,1024]{1,0:T(8,128)S(1)}, f32[16,1024]{1,0:T(8,128)}, u32[]{:S(2)}) copy-start(f32[16,1024]{1,0:T(8,128)} %param.20) | copy-start | bytes 196612
  12.5 17.5 %copy-start.5 = (f32[16,1024]{1,0:T(8,128)S(1)}, f32[16,1024]{1,0:T(8,128)}, u32[]{:S(2)}) copy-start(f32[16,1024]{1,0:T(8,128)} %param.21) | copy-start | bytes 196612
  12.5 227.5 %all-to-all-start = ((bf16[64,2,18,1024]{3,1,2,0:T(2,128)(2,1)}), bf16[64,2,18,1024]{3,1,2,0:T(2,128)(2,1)}, u32[]{:S(2)}, u32[]{:S(2)}) async-start(bf16[64,2,18,1024]{3,1,2,0:T(2,128)(2,1)} %stack.19), calls=%async_computation | async-start | bytes 9437184 | tf_op jit(solution)/shard_map/all_to_all | solution.py:31
  29.5 400.4 %all-gather.2.cloned.1.call-start = ((), (), s32[]{:S(2)}) async-start(), calls=%async_computation.1 | async-start | bytes 8519680 | tf_op jit(solution)/shard_map/all_gather | solution.py:65
  261.8 1.2 copy-start
  306.8 0.7 copy-start.2
  441.5 6.2 %copy-start.1 = (f32[3,2,64,1024]{3,2,1,0:T(8,128)S(1)}, f32[3,2,64,1024]{3,2,1,0:T(8,128)}, u32[]{:S(2)}) copy-start(f32[3,2,64,1024]{3,2,1,0:T(8,128)} %copy-done) | copy-start | bytes 4718596
  441.5 6.2 %copy-start.6 = (f32[1024]{0:T(1024)S(1)}, f32[1024]{0:T(1024)}, u32[]{:S(2)}) copy-start(f32[1024]{0:T(1024)} %param.22) | copy-start | bytes 12292
  447.8 24.3 %copy-start.7 = (f32[1024]{0:T(1024)S(1)}, f32[1024]{0:T(1024)}, u32[]{:S(2)}) copy-start(f32[1024]{0:T(1024)} %param.23) | copy-start | bytes 12292
Sparse Core Ops, SparseCore 0:
  307.6 122.2 all-gather.1
